TPU v7x, 128 devices: a whole 4x4x4 slice. The times are simulated.
128 devices in a mesh: dp: 16 (over y, z), ctx: 8 (over x, core).
Axes of the slice: x: 4, y: 4, z: 4, core: 2. Of those that a mesh axis runs over, the one named last changes fastest.
Arguments:
- input_entries: bfloat16 [16, 2048, 8192], P('dp', 'ctx'), may hold values from -6 to 6
- segment_entry_counts: int32 [16, 8, 8], P('dp'), may hold values from 1 to 64, as said below
- segment_destination_part: int32 [16, 8, 8], P('dp'), may hold values from 0 to 7, as said below
- norm_gain: float32 [8192], replicated, may hold values from 0.25 to 1.75
- kv_weight: bfloat16 [8192, 2048], P('dp'), may hold values from -0.0625 to 0.0625
- kv_bias: float32 [2048], replicated, may hold values from -3 to 3
Outputs:
- evened_residual_entries: bfloat16 [16, 2048, 8192], P('dp', 'ctx')
- lookup_stored_tensors: bfloat16 [16, 2048, 2, 8, 128], P('dp', None, None, 'ctx')
Inputs may be any that keep to these rules, and one draw needn't show every extreme that they name: `segment_entry_counts`: in each sequence the runs of one shard cover its 256 rows; every shard receives exactly 256 rows; at most 64 rows go from one shard to one shard, and every sequence has a run of exactly 64. The numbers of rows between shards form a Latin arrangement: every shard sends the same list of 8 numbers, one to each shard, and receives each number of that list once. `segment_destination_part`: the 8 runs of one shard go to 8 different shards.
All inputs are finite; a program needn't handle non-finite values.
Results may differ from a plain program's by a relative error of at most 0.0046.
Values may be sent and summed in bfloat16 or wider, within the bound.
A program may use at most 192 MiB of HBM per device.

v0:
```python
import jax
import jax.numpy as jnp
from jax import lax
from jax.sharding import PartitionSpec as P

KVH = 8
HD = 128


def plan_tables(lengths, targets, peer_count):
    labels = jnp.arange(peer_count, dtype=jnp.int32)
    starts = jnp.cumsum(lengths, axis=1) - lengths
    matches = (targets[:, :, None] == labels[None, None, :]).astype(jnp.int32)
    counts = jnp.sum(lengths[:, :, None] * matches, axis=1)
    anchors = jnp.sum(starts[:, :, None] * matches, axis=1)
    run_ends = jnp.cumsum(counts, axis=0)
    offsets = run_ends - counts
    return (counts, anchors, offsets, run_ends)


def source_of(positions, ends_column, offsets_column, anchors_column, peer_count):
    labels = jnp.arange(peer_count, dtype=jnp.int32)
    source = jnp.sum((ends_column[None, :] <= positions[:, None]).astype(jnp.int32), axis=1)
    chosen = (source[:, None] == labels[None, :]).astype(jnp.int32)
    within = positions - jnp.sum(chosen * offsets_column[None, :], axis=1)
    anchor = jnp.sum(chosen * anchors_column[None, :], axis=1)
    return (source, within, anchor)


def rms_normed(rows, norm_gain):
    as_float = rows.astype(jnp.float32)
    inverse_rms = lax.rsqrt(jnp.mean(as_float * as_float, axis=-1, keepdims=True) + 1e-06)
    return (as_float * inverse_rms * norm_gain[None, :]).astype(jnp.bfloat16)


def pack_document_runs(rows, counts, anchors, myself, peer_count):
    row_count = rows.shape[0]
    capacity = 2 * row_count // peer_count
    slot_index = jnp.arange(capacity, dtype=jnp.int32)
    my_counts = counts[myself]
    my_anchors = anchors[myself]
    wanted = jnp.minimum(my_anchors[:, None] + slot_index[None, :], row_count - 1)
    is_live = slot_index[None, :] < my_counts[:, None]
    picked = jnp.take(rows, wanted.reshape(-1), axis=0).reshape(peer_count, capacity, -1)
    return jnp.where(is_live[:, :, None], picked, jnp.zeros_like(picked))


def unpack_runs(arriving_rows, positions, run_ends, offsets, anchors, myself, peer_count):
    capacity = arriving_rows.shape[1]
    source, within, anchor = source_of(
        positions, run_ends[:, myself], offsets[:, myself], anchors[:, myself], peer_count
    )
    flat_rows = arriving_rows.reshape(peer_count * capacity, -1)
    return jnp.take(flat_rows, source * capacity + within, axis=0)


def on_device(
    input_entries, segment_entry_counts, segment_destination_part, norm_gain, kv_weight, kv_bias
):
    peer_count = lax.axis_size("ctx")
    myself = lax.axis_index("ctx")
    row_count = input_entries.shape[1]
    counts, anchors, offsets, run_ends = plan_tables(
        segment_entry_counts[0], segment_destination_part[0], peer_count
    )
    positions = jnp.arange(row_count, dtype=jnp.int32)
    outgoing = pack_document_runs(input_entries[0], counts, anchors, myself, peer_count)
    arriving_rows = lax.all_to_all(outgoing, "ctx", split_axis=0, concat_axis=0, tiled=True)
    moved_rows = unpack_runs(
        arriving_rows, positions, run_ends, offsets, anchors, myself, peer_count
    )
    normed = rms_normed(moved_rows, norm_gain)
    summed_squares = jnp.dot(
        normed,
        lax.all_gather(kv_weight, "dp", axis=0, tiled=True),
        preferred_element_type=jnp.float32,
    )
    mapped_outputs = (
        (summed_squares + kv_bias[None, :]).astype(jnp.bfloat16).reshape(1, row_count, 2, KVH, HD)
    )
    by_heads = lax.all_to_all(mapped_outputs, "ctx", split_axis=3, concat_axis=1, tiled=True)
    return (moved_rows[None], by_heads)


def solution(mesh):
    in_specs = (
        P("dp", "ctx", None),
        P("dp", None, None),
        P("dp", None, None),
        P(),
        P("dp", None),
        P(),
    )
    out_specs = (P("dp", "ctx", None), P("dp", None, None, "ctx", None))
    return jax.shard_map(
        on_device, mesh=mesh, in_specs=in_specs, out_specs=out_specs, check_vma=False
    )
```

profile of v0, /device:TPU:1, one launch (start us, length us, event | category | flops | bytes accessed | tf_op | source)
XLA Modules:
  0.0 256.8 jit_solution(8461394061242989045)
XLA Ops:
  7.2 0.0 all-gather.2.cloned.1.call-start
  7.2 0.7 all-gather.2.cloned.1.call-update
  7.9 0.8 reduce_window_sum.23
  8.7 0.7 bitcast_subtract_fusion
  9.4 0.8 select_reduce_fusion.1
  10.3 0.1 add_minimum_fusion
  10.3 0.1 min.22
  10.4 18.2 %gather_fusion = bf16[512,8192]{1,0:T(8,128)(2,1)} fusion(bf16[256,8192]{1,0:T(8,128)(2,1)} %bitcast.28, s32[1024]{0:T(1024)S(1)} %pad_clamp_fusion.1), kind=kCustom, calls=%fused_computation | custom fusion | bytes 16779264 | tf_op jit(solution)/shard_map/jit(_take)/gather | solution.py:44
  28.6 0.1 compare_and_fusion
  28.7 0.1 iota_compare_fusion.3
  28.8 7.6 %select_select_fusion = bf16[8,64,8192]{2,1,0:T(8,128)(2,1)} fusion(bf16[8,64,8192]{2,1,0:T(8,128)(2,1)} %bitcast.29, pred[8,64]{1,0:T(8,128)(4,1)S(1)} %compare_and_fusion, pred[8,64]{1,0:T(8,128)(4,1)S(1)} %iota_compare_fusion.3), kind=kLoop, calls=%fused_computation.7 | loop fusion | flops 8388608 | bytes 16778240 | tf_op jit(solution)/shard_map/jit(_where)/select_n | solution.py:45
  36.4 6.3 %all-to-all-start = ((bf16[8,64,8192]{2,1,0:T(8,128)(2,1)}), bf16[8,64,8192]{2,1,0:T(8,128)(2,1)}, u32[]{:S(2)}, u32[]{:S(2)}) async-start(bf16[8,64,8192]{2,1,0:T(8,128)(2,1)} %select_select_fusion), calls=%async_computation | async-start | bytes 16777216 | tf_op jit(solution)/shard_map/all_to_all | solution.py:68
  42.7 0.2 dynamic-slice_reduce_fusion
  42.9 0.1 convert_reduce_fusion
  43.0 0.1 select_reduce_fusion.2
  43.1 93.4 %all-to-all-done = bf16[8,64,8192]{2,1,0:T(8,128)(2,1)} async-done(((bf16[8,64,8192]{2,1,0:T(8,128)(2,1)}), bf16[8,64,8192]{2,1,0:T(8,128)(2,1)}, u32[]{:S(2)}, u32[]{:S(2)}) %all-to-all-start) | async-done | bytes 8388640 | tf_op jit(solution)/shard_map/all_to_all | solution.py:68
  136.5 13.6 %gather_fusion.1 = bf16[256,8192]{1,0:T(8,128)(2,1)} fusion(bf16[512,8192]{1,0:T(8,128)(2,1)} %bitcast.7, s32[1024]{0:T(1024)S(1)} %pad_clamp_fusion), kind=kCustom, calls=%fused_computation.1 | custom fusion | bytes 8389632 | tf_op jit(solution)/shard_map/jit(_take)/gather | solution.py:54
  150.1 0.0 copy-start
  150.1 0.0 copy-start.1
  150.1 3.4 %fusion = f32[256]{0:T(256)S(1)} fusion(bf16[256,8192]{1,0:T(8,128)(2,1)} %gather_fusion.1, pred[256]{0:T(512)(128)(4,1)S(1)} %compare_and_fusion.1), kind=kLoop, calls=%fused_computation.4 | loop fusion | flops 8388352 | bytes 4195584 | tf_op jit(solution)/shard_map/reduce_sum | solution.py:32
  153.6 57.0 %all-gather.2.cloned.1.call-done = bf16[8192,2048]{1,0:T(8,128)(2,1)} async-done(((bf16[512,2048]{1,0:T(8,128)(2,1)}), bf16[8192,2048]{1,0:T(8,128)(2,1)}) %all-gather.2.cloned.1.call-update) | async-done | bytes 33554448 | tf_op jit(solution)/shard_map/all_gather | solution.py:75
  210.6 0.0 copy-done
  210.6 0.0 copy-done.1
  210.6 16.3 %fusion.13 = bf16[32,8,16,128]{3,1,2,0:T(8,128)(2,1)S(1)} fusion(bf16[8192,2048]{1,0:T(8,128)(2,1)} %all-gather.2.cloned.1.call-done, f32[8192]{0:T(1024)S(1)} %copy-done, f32[256]{0:T(256)S(1)} %add_rsqrt_fusion, bf16[256,8192]{1,0:T(8,128)(2,1)} %gather_fusion.1, pred[256]{0:T(512)(128)(4,1)S(1)} %compare_and_fusion.1, f32[2048]{0:T(1024)S(1)} %copy-done.1), kind=kOutput, calls=%fused_computation.15 | convolution fusion | flops 8601468928 | bytes 38839552 | tf_op jit(solution)/shard_map/dot_general | solution.py:73
  226.9 0.2 copy.14
  227.2 1.8 copy.12
  228.9 4.9 %all-to-all-start.1 = ((bf16[1,256,2,8,128]{4,2,1,0,3:T(2,128)(2,1)}), bf16[1,256,2,8,128]{4,2,1,0,3:T(2,128)(2,1)S(1)}, u32[]{:S(2)}, u32[]{:S(2)}) async-start(bf16[1,256,2,8,128]{4,2,1,0,3:T(2,128)(2,1)} %copy.12), calls=%async_computation.1 | async-start | bytes 2097152 | tf_op jit(solution)/shard_map/all_to_all | solution.py:81
  233.9 4.7 %bitcast_select_fusion = bf16[1,256,8192]{2,1,0:T(8,128)(2,1)} fusion(bf16[256,8192]{1,0:T(8,128)(2,1)} %gather_fusion.1, pred[256]{0:T(512)(128)(4,1)S(1)} %compare_and_fusion.1), kind=kLoop, calls=%fused_computation.9 | loop fusion | flops 2097152 | bytes 8388864 | tf_op jit(solution)/shard_map/jit(_take)/select_n | solution.py:54
  238.5 10.4 %all-to-all-done.1 = bf16[1,256,2,8,128]{4,2,1,0,3:T(2,128)(2,1)S(1)} async-done(((bf16[1,256,2,8,128]{4,2,1,0,3:T(2,128)(2,1)}), bf16[1,256,2,8,128]{4,2,1,0,3:T(2,128)(2,1)S(1)}, u32[]{:S(2)}, u32[]{:S(2)}) %all-to-all-start.1) | async-done | bytes 1048608 | tf_op jit(solution)/shard_map/all_to_all | solution.py:81
  249.0 1.0 copy.16
  (10 shorter events, 0.1 us)
Async XLA Ops:
  7.2 203.4 %all-gather.2.cloned.1.call-start = ((), (), s32[]{:S(2)}) async-start(), calls=%async_computation.2 | async-start | bytes 35651584 | tf_op jit(solution)/shard_map/all_gather | solution.py:75
  36.4 100.2 %all-to-all-start = ((bf16[8,64,8192]{2,1,0:T(8,128)(2,1)}), bf16[8,64,8192]{2,1,0:T(8,128)(2,1)}, u32[]{:S(2)}, u32[]{:S(2)}) async-start(bf16[8,64,8192]{2,1,0:T(8,128)(2,1)} %select_select_fusion), calls=%async_computation | async-start | bytes 16777216 | tf_op jit(solution)/shard_map/all_to_all | solution.py:68
  150.1 60.5 %copy-start = (f32[8192]{0:T(1024)S(1)}, f32[8192]{0:T(1024)}, u32[]{:S(2)}) copy-start(f32[8192]{0:T(1024)} %param.9) | copy-start | bytes 98308
  150.1 60.5 %copy-start.1 = (f32[2048]{0:T(1024)S(1)}, f32[2048]{0:T(1024)}, u32[]{:S(2)}) copy-start(f32[2048]{0:T(1024)} %param.11) | copy-start | bytes 24580
  228.9 20.0 %all-to-all-start.1 = ((bf16[1,256,2,8,128]{4,2,1,0,3:T(2,128)(2,1)}), bf16[1,256,2,8,128]{4,2,1,0,3:T(2,128)(2,1)S(1)}, u32[]{:S(2)}, u32[]{:S(2)}) async-start(bf16[1,256,2,8,128]{4,2,1,0,3:T(2,128)(2,1)} %copy.12), calls=%async_computation.1 | async-start | bytes 2097152 | tf_op jit(solution)/shard_map/all_to_all | solution.py:81
Sparse Core Ops, SparseCore 0:
  10.1 200.4 all-gather.1
where the time goes:
time: 257 us
  waiting for transfers between devices  162 us (63%)
  local copies, waits for them, and re-layouts  35.1 us (14%)
  other arithmetic  18.5 us (7%)
  matrix products  16.3 us (6%)
  between operations  14.1 us (5%)
  starting transfers between devices  11.3 us (4%)
    all_to_all x1, waiting for transfers between devices, on_device(): lax.all_to_all(outgoing, 'ctx', split_axis=0, concat_axis=0, tiled=True)  93.4 us
    all_gather x1, waiting for transfers between devices, on_device(): lax.all_gather(kv_weight, 'dp', axis=0, tiled=True)  57 us
    gather x1, local copies, waits for them, and re-layouts, pack_document_runs(): jnp.take(rows, wanted.reshape(-1), axis=0).reshape(peer_count, capacity, -1)  18.2 us
    dot_general x1, matrix products, on_device(): jnp.dot(normed, lax.all_gather(kv_weight, 'dp', axis=0, tiled=True), pref...  16.3 us
    gather x1, local copies, waits for them, and re-layouts, unpack_runs(): return jnp.take(flat_rows, source * capacity + within, axis=0)  13.6 us
    all_to_all x1, waiting for transfers between devices, on_device(): lax.all_to_all(mapped_outputs, 'ctx', split_axis=3, concat_axis=1, tiled=...  10.4 us
    select_n x1, other arithmetic, pack_document_runs(): return jnp.where(is_live[:, :, None], picked, jnp.zeros_like(picked))  7.59 us
    all_to_all x1, starting transfers between devices, on_device(): lax.all_to_all(outgoing, 'ctx', split_axis=0, concat_axis=0, tiled=True)  6.29 us
  transfers between devices with their start and end apart: 3, of which 3 were waited for; matrix products, arithmetic and copies ran while one was open for 20% of the time, Pallas kernels for 0%

commit v1 on v0

--- a/solution.py
+++ b/solution.py
@@ -5,6 +5,22 @@
 
 KVH = 8
 HD = 128
+
+
+def swapped_with_each(x, axis, split, join):
+    ways, here = (lax.axis_size(axis), lax.axis_index(axis))
+    width = x.shape[split] // ways
+    shape = list(x.shape)
+    shape[split] = width
+    height = shape[join]
+    shape[join] = height * ways
+    full = jnp.zeros(shape, x.dtype)
+    for mask in range(ways):
+        part = lax.dynamic_slice_in_dim(x, (here ^ mask) * width, width, axis=split)
+        if mask:
+            part = lax.ppermute(part, axis, [(d, d ^ mask) for d in range(ways)])
+        full = lax.dynamic_update_slice_in_dim(full, part, (here ^ mask) * height, axis=join)
+    return full
 
 
 def plan_tables(lengths, targets, peer_count):
@@ -78,7 +94,7 @@
     mapped_outputs = (
         (summed_squares + kv_bias[None, :]).astype(jnp.bfloat16).reshape(1, row_count, 2, KVH, HD)
     )
-    by_heads = lax.all_to_all(mapped_outputs, "ctx", split_axis=3, concat_axis=1, tiled=True)
+    by_heads = swapped_with_each(mapped_outputs, "ctx", 3, 1)
     return (moved_rows[None], by_heads)
 
 

time: 257 us -> 260 us (1.012)
  starting transfers between devices: 11.3 us -> 15.4 us
  waiting for transfers between devices: 162 us -> 159 us
  local copies, waits for them, and re-layouts: 35.1 us -> 37.7 us
    ppermute x0 -> x7, waiting for transfers between devices: none -> 11.1 us  [swapped_with_each(): part = lax.ppermute(part, axis, [(d, d ^ mask) for d in range(ways)])]
    all_to_all x1 -> x0, waiting for transfers between devices: 10.4 us -> none  [on_device(): lax.all_to_all(mapped_outputs, 'ctx', split_axis=3, concat_axis=1, tiled=...]
    ppermute x0 -> x7, starting transfers between devices: none -> 9.09 us  [swapped_with_each(): part = lax.ppermute(part, axis, [(d, d ^ mask) for d in range(ways)])]
    all_to_all x1 -> x0, starting transfers between devices: 4.93 us -> none  [on_device(): lax.all_to_all(mapped_outputs, 'ctx', split_axis=3, concat_axis=1, tiled=...]
  transfers between devices with their start and end apart: 3 -> 9, of which waited for: 3 -> 6; matrix products, arithmetic and copies ran while one was open for 20% -> 19% of each run, Pallas kernels for 0% -> 0%
where the time goes in v1:
time: 260 us
  waiting for transfers between devices  159 us (61%)
  local copies, waits for them, and re-layouts  37.7 us (15%)
  other arithmetic  16.5 us (6%)
  matrix products  16.4 us (6%)
  starting transfers between devices  15.4 us (6%)
  between operations  14.4 us (6%)
    all_to_all x1, waiting for transfers between devices, on_device(): lax.all_to_all(outgoing, 'ctx', split_axis=0, concat_axis=0, tiled=True)  93.3 us
    all_gather x1, waiting for transfers between devices, on_device(): lax.all_gather(kv_weight, 'dp', axis=0, tiled=True)  54.5 us
    gather x1, local copies, waits for them, and re-layouts, pack_document_runs(): jnp.take(rows, wanted.reshape(-1), axis=0).reshape(peer_count, capacity, -1)  18.2 us
    dot_general x1, matrix products, on_device(): jnp.dot(normed, lax.all_gather(kv_weight, 'dp', axis=0, tiled=True), pref...  16.4 us
    gather x1, local copies, waits for them, and re-layouts, unpack_runs(): return jnp.take(flat_rows, source * capacity + within, axis=0)  13.5 us
    ppermute x7, waiting for transfers between devices, swapped_with_each(): part = lax.ppermute(part, axis, [(d, d ^ mask) for d in range(ways)])  11.1 us
    ppermute x7, starting transfers between devices, swapped_with_each(): part = lax.ppermute(part, axis, [(d, d ^ mask) for d in range(ways)])  9.09 us
    select_n x1, other arithmetic, pack_document_runs(): return jnp.where(is_live[:, :, None], picked, jnp.zeros_like(picked))  7.59 us
  transfers between devices with their start and end apart: 9, of which 6 were waited for; matrix products, arithmetic and copies ran while one was open for 19% of the time, Pallas kernels for 0%

profile of v1, /device:TPU:1, one launch (start us, length us, event | category | flops | bytes accessed | tf_op | source)
XLA Modules:
  0.0 259.9 jit_solution(11941559758508850577)
XLA Ops:
  7.2 0.7 all-gather.2.cloned.1.call-update
  7.9 0.8 reduce_window_sum.23
  8.7 0.7 bitcast_subtract_fusion
  9.4 0.8 select_reduce_fusion.1
  10.4 18.2 %gather_fusion = bf16[512,8192]{1,0:T(8,128)(2,1)} fusion(bf16[256,8192]{1,0:T(8,128)(2,1)} %bitcast.21, s32[1024]{0:T(1024)S(1)} %pad_clamp_fusion.1), kind=kCustom, calls=%fused_computation | custom fusion | bytes 16779264 | tf_op jit(solution)/shard_map/jit(_take)/gather | solution.py:60
  28.8 7.6 %select_select_fusion = bf16[8,64,8192]{2,1,0:T(8,128)(2,1)} fusion(bf16[8,64,8192]{2,1,0:T(8,128)(2,1)} %bitcast.22, pred[8,64]{1,0:T(8,128)(4,1)S(1)} %compare_and_fusion, pred[8,64]{1,0:T(8,128)(4,1)S(1)} %iota_compare_fusion.3), kind=kLoop, calls=%fused_computation.7 | loop fusion | flops 8388608 | bytes 16778240 | tf_op jit(solution)/shard_map/jit(_where)/select_n | solution.py:61
  36.4 6.3 %all-to-all-start = ((bf16[8,64,8192]{2,1,0:T(8,128)(2,1)}), bf16[8,64,8192]{2,1,0:T(8,128)(2,1)}, u32[]{:S(2)}, u32[]{:S(2)}) async-start(bf16[8,64,8192]{2,1,0:T(8,128)(2,1)} %select_select_fusion), calls=%async_computation | async-start | bytes 16777216 | tf_op jit(solution)/shard_map/all_to_all | solution.py:84
  42.8 0.2 fusion.16
  43.3 93.3 %all-to-all-done = bf16[8,64,8192]{2,1,0:T(8,128)(2,1)} async-done(((bf16[8,64,8192]{2,1,0:T(8,128)(2,1)}), bf16[8,64,8192]{2,1,0:T(8,128)(2,1)}, u32[]{:S(2)}, u32[]{:S(2)}) %all-to-all-start) | async-done | bytes 8388640 | tf_op jit(solution)/shard_map/all_to_all | solution.py:84
  136.5 13.5 %gather_fusion.1 = bf16[256,8192]{1,0:T(8,128)(2,1)} fusion(bf16[512,8192]{1,0:T(8,128)(2,1)} %bitcast.7, s32[1024]{0:T(1024)S(1)} %pad_clamp_fusion), kind=kCustom, calls=%fused_computation.1 | custom fusion | bytes 8389632 | tf_op jit(solution)/shard_map/jit(_take)/gather | solution.py:70
  150.0 3.6 %fusion = f32[256]{0:T(256)S(1)} fusion(bf16[256,8192]{1,0:T(8,128)(2,1)} %gather_fusion.1, pred[256]{0:T(512)(128)(4,1)S(1)} %compare_and_fusion.1), kind=kLoop, calls=%fused_computation.4 | loop fusion | flops 8388352 | bytes 4195584 | tf_op jit(solution)/shard_map/reduce_sum | solution.py:48
  153.6 2.5 bitcast_select_fusion
  156.1 54.5 %all-gather.2.cloned.1.call-done = bf16[8192,2048]{1,0:T(8,128)(2,1)} async-done(((bf16[512,2048]{1,0:T(8,128)(2,1)}), bf16[8192,2048]{1,0:T(8,128)(2,1)}) %all-gather.2.cloned.1.call-update) | async-done | bytes 33554448 | tf_op jit(solution)/shard_map/all_gather | solution.py:91
  210.6 16.4 %fusion.13 = bf16[32,8,16,128]{3,1,2,0:T(8,128)(2,1)S(1)} fusion(bf16[8192,2048]{1,0:T(8,128)(2,1)} %all-gather.2.cloned.1.call-done, f32[8192]{0:T(1024)S(1)} %copy-done.2, f32[256]{0:T(256)S(1)} %add_rsqrt_fusion, bf16[256,8192]{1,0:T(8,128)(2,1)} %gather_fusion.1, pred[256]{0:T(512)(128)(4,1)S(1)} %compare_and_fusion.1, f32[2048]{0:T(1024)S(1)} %copy-done.3), kind=kOutput, calls=%fused_computation.15 | convolution fusion | flops 8601468928 | bytes 38839552 | tf_op jit(solution)/shard_map/dot_general | solution.py:89
  227.0 0.2 copy.40
  227.3 2.4 constant_dynamic-slice_fusion
  229.8 0.8 collective-permute-start
  230.7 1.3 collective-permute-start.1
  232.0 0.6 collective-permute-start.2
  232.7 2.8 %collective-permute-start.3 = (bf16[1,256,2,1,128]{4,2,3,1,0:T(2,128)(2,1)S(1)}, bf16[1,256,2,1,128]{4,2,3,1,0:T(2,128)(2,1)S(1)}, u32[]{:S(2)}, u32[]{:S(2)}) collective-permute-start(bf16[1,256,2,1,128]{4,2,3,1,0:T(2,128)(2,1)S(1)} %copy.36), channel_id=1, source_target_pairs={{0,4},{1,5},{2,6},{3,7},{4,0},{5,1},{6,2},{7,3},{8,12},{9,13},{10,... | collective-permute-start | bytes 393224 | tf_op jit(solution)/shard_map/ppermute | solution.py:21
  235.5 0.7 collective-permute-start.4
  236.3 0.6 broadcast_in_dim.56
  237.2 2.5 collective-permute-start.5
  239.6 0.1 constant_dynamic-update-slice_fusion.6
  239.8 0.5 collective-permute-start.6
  240.4 0.1 constant_dynamic-update-slice_fusion.4
  240.5 3.1 %collective-permute-done.3 = bf16[1,256,2,1,128]{4,2,3,1,0:T(2,128)(2,1)S(1)} collective-permute-done((bf16[1,256,2,1,128]{4,2,3,1,0:T(2,128)(2,1)S(1)}, bf16[1,256,2,1,128]{4,2,3,1,0:T(2,128)(2,1)S(1)}, u32[]{:S(2)}, u32[]{:S(2)}) %collective-permute-start.3) | collective-permute-done | bytes 131104 | tf_op jit(solution)/shard_map/ppermute | solution.py:21
  243.8 2.9 %collective-permute-done.4 = bf16[1,256,2,1,128]{4,2,3,1,0:T(2,128)(2,1)S(1)} collective-permute-done((bf16[1,256,2,1,128]{4,2,3,1,0:T(2,128)(2,1)S(1)}, bf16[1,256,2,1,128]{4,2,3,1,0:T(2,128)(2,1)S(1)}, u32[]{:S(2)}, u32[]{:S(2)}) %collective-permute-start.4) | collective-permute-done | bytes 131104 | tf_op jit(solution)/shard_map/ppermute | solution.py:21
  246.7 2.4 collective-permute-done.5
  249.3 2.7 %collective-permute-done.6 = bf16[1,256,2,1,128]{4,2,3,1,0:T(2,128)(2,1)S(1)} collective-permute-done((bf16[1,256,2,1,128]{4,2,3,1,0:T(2,128)(2,1)S(1)}, bf16[1,256,2,1,128]{4,2,3,1,0:T(2,128)(2,1)S(1)}, u32[]{:S(2)}, u32[]{:S(2)}) %collective-permute-start.6) | collective-permute-done | bytes 131104 | tf_op jit(solution)/shard_map/ppermute | solution.py:21
  251.9 0.1 constant_dynamic-update-slice_fusion
  252.1 1.0 copy-done.1
  (39 shorter events, 1.8 us)
Async XLA Ops:
  7.2 203.4 %all-gather.2.cloned.1.call-start = ((), (), s32[]{:S(2)}) async-start(), calls=%async_computation.1 | async-start | bytes 35651584 | tf_op jit(solution)/shard_map/all_gather | solution.py:91
  36.4 100.2 %all-to-all-start = ((bf16[8,64,8192]{2,1,0:T(8,128)(2,1)}), bf16[8,64,8192]{2,1,0:T(8,128)(2,1)}, u32[]{:S(2)}, u32[]{:S(2)}) async-start(bf16[8,64,8192]{2,1,0:T(8,128)(2,1)} %select_select_fusion), calls=%async_computation | async-start | bytes 16777216 | tf_op jit(solution)/shard_map/all_to_all | solution.py:84
  150.0 3.6 %copy-start = (bf16[256,8192]{1,0:T(8,128)(2,1)S(1)}, bf16[256,8192]{1,0:T(8,128)(2,1)}, u32[]{:S(2)}) copy-start(bf16[256,8192]{1,0:T(8,128)(2,1)} %gather_fusion.1) | copy-start | bytes 12582916
  153.6 57.0 %copy-start.2 = (f32[8192]{0:T(1024)S(1)}, f32[8192]{0:T(1024)}, u32[]{:S(2)}) copy-start(f32[8192]{0:T(1024)} %param.9) | copy-start | bytes 98308
  153.6 57.0 %copy-start.3 = (f32[2048]{0:T(1024)S(1)}, f32[2048]{0:T(1024)}, u32[]{:S(2)}) copy-start(f32[2048]{0:T(1024)} %param.11) | copy-start | bytes 24580
  229.8 7.3 %collective-permute-start = (bf16[1,256,2,1,128]{4,2,3,1,0:T(2,128)(2,1)S(1)}, bf16[1,256,2,1,128]{4,2,3,1,0:T(2,128)(2,1)S(1)}, u32[]{:S(2)}, u32[]{:S(2)}) collective-permute-start(bf16[1,256,2,1,128]{4,2,3,1,0:T(2,128)(2,1)S(1)} %copy.33), channel_id=1, source_target_pairs={{0,1},{1,0},{2,3},{3,2},{4,5},{5,4},{6,7},{7,6},{8,9},{9,8},{10,11... | collective-permute-start | bytes 393224 | tf_op jit(solution)/shard_map/ppermute | solution.py:21
  230.7 9.1 %collective-permute-start.1 = (bf16[1,256,2,1,128]{4,2,3,1,0:T(2,128)(2,1)S(1)}, bf16[1,256,2,1,128]{4,2,3,1,0:T(2,128)(2,1)S(1)}, u32[]{:S(2)}, u32[]{:S(2)}) collective-permute-start(bf16[1,256,2,1,128]{4,2,3,1,0:T(2,128)(2,1)S(1)} %copy.34), channel_id=1, source_target_pairs={{0,2},{1,3},{2,0},{3,1},{4,6},{5,7},{6,4},{7,5},{8,10},{9,11},{10,... | collective-permute-start | bytes 393224 | tf_op jit(solution)/shard_map/ppermute | solution.py:21
  232.0 8.4 %collective-permute-start.2 = (bf16[1,256,2,1,128]{4,2,3,1,0:T(2,128)(2,1)S(1)}, bf16[1,256,2,1,128]{4,2,3,1,0:T(2,128)(2,1)S(1)}, u32[]{:S(2)}, u32[]{:S(2)}) collective-permute-start(bf16[1,256,2,1,128]{4,2,3,1,0:T(2,128)(2,1)S(1)} %copy.35), channel_id=1, source_target_pairs={{0,3},{1,2},{2,1},{3,0},{4,7},{5,6},{6,5},{7,4},{8,11},{9,10},{10,... | collective-permute-start | bytes 393224 | tf_op jit(solution)/shard_map/ppermute | solution.py:21
  232.7 11.0 %collective-permute-start.3 = (bf16[1,256,2,1,128]{4,2,3,1,0:T(2,128)(2,1)S(1)}, bf16[1,256,2,1,128]{4,2,3,1,0:T(2,128)(2,1)S(1)}, u32[]{:S(2)}, u32[]{:S(2)}) collective-permute-start(bf16[1,256,2,1,128]{4,2,3,1,0:T(2,128)(2,1)S(1)} %copy.36), channel_id=1, source_target_pairs={{0,4},{1,5},{2,6},{3,7},{4,0},{5,1},{6,2},{7,3},{8,12},{9,13},{10,... | collective-permute-start | bytes 393224 | tf_op jit(solution)/shard_map/ppermute | solution.py:21
  235.5 11.1 %collective-permute-start.4 = (bf16[1,256,2,1,128]{4,2,3,1,0:T(2,128)(2,1)S(1)}, bf16[1,256,2,1,128]{4,2,3,1,0:T(2,128)(2,1)S(1)}, u32[]{:S(2)}, u32[]{:S(2)}) collective-permute-start(bf16[1,256,2,1,128]{4,2,3,1,0:T(2,128)(2,1)S(1)} %copy.37), channel_id=1, source_target_pairs={{0,5},{1,4},{2,7},{3,6},{4,1},{5,0},{6,3},{7,2},{8,13},{9,12},{10,... | collective-permute-start | bytes 393224 | tf_op jit(solution)/shard_map/ppermute | solution.py:21
  237.2 12.0 %collective-permute-start.5 = (bf16[1,256,2,1,128]{4,2,3,1,0:T(2,128)(2,1)S(1)}, bf16[1,256,2,1,128]{4,2,3,1,0:T(2,128)(2,1)S(1)}, u32[]{:S(2)}, u32[]{:S(2)}) collective-permute-start(bf16[1,256,2,1,128]{4,2,3,1,0:T(2,128)(2,1)S(1)} %copy.38), channel_id=1, source_target_pairs={{0,6},{1,7},{2,4},{3,5},{4,2},{5,3},{6,0},{7,1},{8,14},{9,15},{10,... | collective-permute-start | bytes 393224 | tf_op jit(solution)/shard_map/ppermute | solution.py:21
  239.8 12.2 %collective-permute-start.6 = (bf16[1,256,2,1,128]{4,2,3,1,0:T(2,128)(2,1)S(1)}, bf16[1,256,2,1,128]{4,2,3,1,0:T(2,128)(2,1)S(1)}, u32[]{:S(2)}, u32[]{:S(2)}) collective-permute-start(bf16[1,256,2,1,128]{4,2,3,1,0:T(2,128)(2,1)S(1)} %copy.39), channel_id=1, source_target_pairs={{0,7},{1,6},{2,5},{3,4},{4,3},{5,2},{6,1},{7,0},{8,15},{9,14},{10,... | collective-permute-start | bytes 393224 | tf_op jit(solution)/shard_map/ppermute | solution.py:21
  252.1 1.0 copy-start.1
Sparse Core Ops, SparseCore 0:
  10.1 200.4 all-gather.1
